TPU v7x, 512 devices: a whole 4x8x8 slice. The times are simulated.
512 devices in a mesh: seq: 128 (over y, x_lo, z), ch: 4 (over x_hi, core).
Axes of the slice: x: 4 (x_hi: 2, x_lo: 2; x = x_hi * 2 + x_lo), y: 8, z: 8, core: 2. Of those that a mesh axis runs over, the one named last changes fastest.
Arguments:
- signal_x: bfloat16 [64, 65536], P('ch', 'seq'), may hold values from -6 to 6
- gate_q: bfloat16 [64, 65536], P('ch', 'seq'), may hold values from -6 to 6
- gate_k: bfloat16 [64, 65536], P('ch', 'seq'), may hold values from -6 to 6
- skip_gain: float32 [64], P('ch'), may hold values from 0.5 to 1.5
- residue: float32 [16], replicated, may hold values from -1.5 to 1.5
- memory: float32 [16], replicated, may hold values from 30 to 262144
- cotangent: bfloat16 [64, 65536], P('ch', 'seq'), may hold values from -6 to 6
Outputs:
- output: bfloat16 [64, 65536], P('ch', 'seq')
- grad_x: bfloat16 [64, 65536], P('ch', 'seq')
- grad_q: bfloat16 [64, 65536], P('ch', 'seq')
- grad_k: bfloat16 [64, 65536], P('ch', 'seq')
- grad_skip: float32 [64], P('ch')
- grad_residue: float32 [16], replicated
- grad_memory: float32 [16], replicated
All inputs are finite; a program needn't handle non-finite values.
Results may differ from a plain program's by a relative error of at most 0.002.
Values sent between devices are 32-bit elements; how exact they have to be, the bound alone decides.
A program may use at most 64 MiB of HBM per device.

v0:
```python
import math
import jax
import jax.numpy as jnp
from jax import lax
from jax.sharding import PartitionSpec as P

HIGH_PREC = lax.Precision.HIGHEST


def partner_2(shard, axis, stride):
    return lax.ppermute(shard, axis, [(i, i ^ 1 << stride) for i in range(lax.axis_size(axis))])


def cmul(left_op, right_op):
    return jnp.stack(
        [
            left_op[0] * right_op[0] - left_op[1] * right_op[1],
            left_op[0] * right_op[1] + left_op[1] * right_op[0],
        ]
    )


def dft_pair(order_len, orient):
    indices = jnp.arange(order_len, dtype=jnp.int32)
    products = indices[:, None] * indices[None, :] % order_len
    angles = products.astype(jnp.float32) * (2.0 * math.pi / order_len)
    return (jnp.cos(angles), orient * jnp.sin(angles))


def apply_matrix(signal_data, matrix_pair, pattern):
    with_cos = jnp.einsum(pattern, signal_data, matrix_pair[0], precision=HIGH_PREC)
    with_sin = jnp.einsum(pattern, signal_data, matrix_pair[1], precision=HIGH_PREC)
    return jnp.stack([with_cos[0] - with_sin[1], with_sin[0] + with_cos[1]])


def split_factor(local_len):
    chosen = 1
    factor = 1
    while factor * factor <= local_len:
        if local_len % factor == 0:
            chosen = factor
        factor = factor + 1
    return chosen


def inner_twiddle(outer_len, inner_len, orient):
    local_len = outer_len * inner_len
    rows_idx = jnp.arange(outer_len, dtype=jnp.int32)
    cols_idx = jnp.arange(inner_len, dtype=jnp.int32)
    products = rows_idx[:, None] * cols_idx[None, :] % local_len
    angles = products.astype(jnp.float32) * (2.0 * math.pi / local_len)
    return jnp.stack([jnp.cos(angles), orient * jnp.sin(angles)])[:, None, None]


def local_forward(signal_data):
    local_len = signal_data.shape[-1]
    outer_len = split_factor(local_len)
    inner_len = local_len // outer_len
    shaped = signal_data.reshape(signal_data.shape[:3] + (outer_len, inner_len))
    shaped = apply_matrix(shaped, dft_pair(outer_len, -1.0), "zsxab,ak->zsxkb")
    shaped = cmul(shaped, inner_twiddle(outer_len, inner_len, -1.0))
    shaped = apply_matrix(shaped, dft_pair(inner_len, -1.0), "zsxkb,bc->zsxkc")
    return shaped.reshape(signal_data.shape)


def local_inverse(signal_data):
    local_len = signal_data.shape[-1]
    outer_len = split_factor(local_len)
    inner_len = local_len // outer_len
    shaped = signal_data.reshape(signal_data.shape[:3] + (outer_len, inner_len))
    shaped = apply_matrix(shaped, dft_pair(inner_len, 1.0), "zsxkc,cb->zsxkb")
    shaped = cmul(shaped, inner_twiddle(outer_len, inner_len, 1.0))
    shaped = apply_matrix(shaped, dft_pair(outer_len, 1.0), "zsxkb,kj->zsxjb")
    return shaped.reshape(signal_data.shape)


def global_twiddle(freq_block, local_len, full_len, orient):
    slot_ids = jnp.arange(2, dtype=jnp.int32)
    freq_ids = 2 * freq_block + slot_ids
    products = freq_ids[:, None] * jnp.arange(local_len, dtype=jnp.int32)[None, :]
    angles = products.astype(jnp.float32) * (2.0 * math.pi / full_len)
    return jnp.stack([jnp.cos(angles), orient * jnp.sin(angles)])[:, None]


def bit_reverse(seq_index, sections):
    reversed_idx = jnp.zeros((), jnp.int32)
    for bit_level in range(sections):
        reversed_idx = reversed_idx | (seq_index >> bit_level & 1) << sections - 1 - bit_level
    return reversed_idx


def level_weight(seq_index, bit_level, orient):
    offset = seq_index & (1 << bit_level) - 1
    angles = offset.astype(jnp.float32) * (2.0 * math.pi / 2 ** (bit_level + 1))
    is_upper = seq_index >> bit_level & 1
    return (jnp.stack([jnp.cos(angles), orient * jnp.sin(angles)]), is_upper)


def forward_partners(signal_data, sections):
    seq_index = lax.axis_index("seq")
    for bit_level in range(sections - 1, -1, -1):
        partner = partner_2(signal_data, "seq", bit_level)
        weight, is_upper = level_weight(seq_index, bit_level, -1.0)
        summed = signal_data + partner
        differ = cmul(partner - signal_data, weight)
        signal_data = jnp.where(is_upper == 1, differ, summed)
    return signal_data


def inverse_partners(signal_data, sections):
    seq_index = lax.axis_index("seq")
    for bit_level in range(sections):
        partner = partner_2(signal_data, "seq", bit_level)
        weight, is_upper = level_weight(seq_index, bit_level, 1.0)
        lower_new = signal_data + cmul(partner, weight)
        upper_new = partner - cmul(signal_data, weight)
        signal_data = jnp.where(is_upper == 1, upper_new, lower_new)
    return signal_data


def forward_transform(signals, sections):
    seq_index = lax.axis_index("seq")
    devices = lax.axis_size("seq")
    local_len = signals.shape[-1]
    full_len = 2 * devices * local_len
    angles = seq_index.astype(jnp.float32) * (math.pi / devices)
    weight = jnp.stack([jnp.cos(angles), -jnp.sin(angles)])
    signal_data = jnp.stack([signals, cmul(signals, weight)], axis=2)
    signal_data = forward_partners(signal_data, sections)
    freq_block = bit_reverse(seq_index, sections)
    signal_data = cmul(signal_data, global_twiddle(freq_block, local_len, full_len, -1.0))
    return local_forward(signal_data)


def inverse_transform(spectra, sections):
    seq_index = lax.axis_index("seq")
    devices = lax.axis_size("seq")
    local_len = spectra.shape[-1]
    full_len = 2 * devices * local_len
    signal_data = local_inverse(spectra)
    freq_block = bit_reverse(seq_index, sections)
    signal_data = cmul(signal_data, global_twiddle(freq_block, local_len, full_len, 1.0))
    signal_data = inverse_partners(signal_data, sections)
    angles = seq_index.astype(jnp.float32) * (math.pi / devices)
    weight = jnp.stack([jnp.cos(angles), jnp.sin(angles)])
    result = signal_data[:, :, 0] + cmul(signal_data[:, :, 1], weight)
    return result / full_len


def per_device(signal_x, gate_q, gate_k, skip_gain, residue, memory, cotangent):
    channels, local_len = signal_x.shape
    devices = lax.axis_size("seq")
    sections = devices.bit_length() - 1
    seq_index = lax.axis_index("seq")
    positions = (seq_index * local_len + jnp.arange(local_len, dtype=jnp.int32)).astype(jnp.float32)
    weights = jnp.sqrt(2.0 / memory)[:, None] * jnp.exp(-positions[None, :] / memory[:, None])
    filter_taps = jnp.sum(residue[:, None] * weights, axis=0)
    x_float = signal_x.astype(jnp.float32)
    q_float = gate_q.astype(jnp.float32)
    k_float = gate_k.astype(jnp.float32)
    d_float = cotangent.astype(jnp.float32)
    values = x_float * k_float
    grad_mixed = d_float * q_float
    value_sig = jnp.stack([values, jnp.zeros_like(values)])
    grad_sig = jnp.stack([grad_mixed, jnp.zeros_like(grad_mixed)])
    sig_count = value_sig.shape[1]
    taps_sig = jnp.stack([filter_taps, jnp.zeros_like(filter_taps)])[:, None]
    spectra = forward_transform(jnp.concatenate([value_sig, taps_sig], axis=1), sections)
    value_spec = spectra[:, :sig_count]
    taps_spec = spectra[:, sig_count:]
    conv_sig = inverse_transform(cmul(value_spec, taps_spec), sections)
    grad_spec = forward_transform(grad_sig, sections)
    conj_sign = jnp.array([1.0, -1.0], jnp.float32).reshape(2, 1, 1, 1)
    back_spec = cmul(taps_spec * conj_sign, grad_spec)
    cross_spec = jnp.sum(cmul(value_spec * conj_sign, grad_spec), axis=1, keepdims=True)
    back_sig = inverse_transform(jnp.concatenate([back_spec, cross_spec], axis=1), sections)
    grad_taps = back_sig[0, sig_count]
    conv_out = conv_sig[0]
    corr_out = back_sig[0, :sig_count]
    mixed_out = conv_out + skip_gain[:, None] * values
    output = (q_float * mixed_out).astype(jnp.bfloat16)
    grad_values = skip_gain[:, None] * grad_mixed + corr_out
    grad_x = (grad_values * k_float).astype(jnp.bfloat16)
    grad_q = (d_float * mixed_out).astype(jnp.bfloat16)
    grad_k = (grad_values * x_float).astype(jnp.bfloat16)
    weighted = weights * grad_taps[None, :]
    part_residue = jnp.sum(weighted, axis=1)
    part_memory = residue * jnp.sum(weighted * (positions[None, :] / memory[:, None] - 0.5), axis=1)
    part_skip = jnp.sum(grad_mixed * values, axis=1)
    all_channels = channels * lax.axis_size("ch")
    seq_total = devices * local_len
    sum_residue, sum_memory = lax.psum((part_residue, part_memory), ("seq", "ch"))
    sum_skip = lax.psum(part_skip, "seq")
    norm_scale = 1.0 / math.sqrt(all_channels * seq_total)
    grad_skip = sum_skip / math.sqrt(seq_total)
    grad_residue = sum_residue * norm_scale
    grad_memory = sum_memory * norm_scale
    return (output, grad_x, grad_q, grad_k, grad_skip, grad_residue, grad_memory)


def solution(mesh):
    return jax.shard_map(
        per_device,
        mesh=mesh,
        in_specs=(
            P("ch", "seq"),
            P("ch", "seq"),
            P("ch", "seq"),
            P("ch"),
            P(),
            P(),
            P("ch", "seq"),
        ),
        out_specs=(
            P("ch", "seq"),
            P("ch", "seq"),
            P("ch", "seq"),
            P("ch", "seq"),
            P("ch"),
            P(),
            P(),
        ),
        check_vma=False,
    )
```

profile of v0, /device:TPU:4, one launch (start us, length us, event | category | flops | bytes accessed | tf_op | source)
XLA Modules:
  0.0 616.5 jit_solution(16483242981298394517)
XLA Ops:
  0.8 0.6 copy-done.6
  2.3 7.7 %collective-permute-start = (f32[2,17,2,512]{3,1,2,0:T(8,128)S(1)}, f32[2,17,2,512]{3,1,2,0:T(8,128)S(1)}, u32[]{:S(2)}, u32[]{:S(2)}) collective-permute-start(f32[2,17,2,512]{3,1,2,0:T(8,128)S(1)} %pad_maximum_fusion.13), channel_id=1, source_target_pairs={{0,256},{4,260},{8,264},{12,268},{16,272},{20,276},{24,280},{28,28... | collective-permute-start | bytes 417800 | tf_op jit(solution)/shard_map/ppermute | solution.py:11
  10.1 2.0 collective-permute-start.14
  13.4 10.8 %collective-permute-done.14 = f32[2,16,2,512]{3,1,0,2:T(8,128)S(1)} collective-permute-done((f32[2,16,2,512]{3,1,0,2:T(8,128)S(1)}, f32[2,16,2,512]{3,1,0,2:T(8,128)S(1)}, u32[]{:S(2)}, u32[]{:S(2)}) %collective-permute-start.14) | collective-permute-done | bytes 131104 | tf_op jit(solution)/shard_map/ppermute | solution.py:11
  24.4 4.9 collective-permute-start.15
  29.4 1.9 collective-permute-start.1
  31.4 7.9 %collective-permute-done.15 = f32[2,16,2,512]{3,1,0,2:T(8,128)S(1)} collective-permute-done((f32[2,16,2,512]{3,1,0,2:T(8,128)S(1)}, f32[2,16,2,512]{3,1,0,2:T(8,128)S(1)}, u32[]{:S(2)}, u32[]{:S(2)}) %collective-permute-start.15) | collective-permute-done | bytes 131104 | tf_op jit(solution)/shard_map/ppermute | solution.py:11
  39.4 1.9 collective-permute-start.16
  41.3 1.8 collective-permute-done.1
  43.3 2.1 collective-permute-start.2
  45.5 0.8 collective-permute-done.16
  46.3 3.1 collective-permute-start.17
  49.4 2.4 collective-permute-done.2
  51.9 3.1 collective-permute-start.3
  55.1 10.9 %collective-permute-start.18 = (f32[2,16,2,512]{3,1,0,2:T(8,128)S(1)}, f32[2,16,2,512]{3,1,0,2:T(8,128)S(1)}, u32[]{:S(2)}, u32[]{:S(2)}) collective-permute-start(f32[2,16,2,512]{3,1,0,2:T(8,128)S(1)} %maximum_select_fusion.10), channel_id=1, source_target_pairs={{0,16},{4,20},{8,24},{12,28},{16,0},{20,4},{24,8},{28,12},{32,48},... | collective-permute-start | bytes 393224 | tf_op jit(solution)/shard_map/ppermute | solution.py:11
  66.2 4.3 collective-permute-start.4
  70.8 7.4 %collective-permute-start.19 = (f32[2,16,2,512]{3,1,0,2:T(8,128)S(1)}, f32[2,16,2,512]{3,1,0,2:T(8,128)S(1)}, u32[]{:S(2)}, u32[]{:S(2)}) collective-permute-start(f32[2,16,2,512]{3,1,0,2:T(8,128)S(1)} %maximum_select_fusion.11), channel_id=1, source_target_pairs={{0,8},{4,12},{8,0},{12,4},{16,24},{20,28},{24,16},{28,20},{32,40},... | collective-permute-start | bytes 393224 | tf_op jit(solution)/shard_map/ppermute | solution.py:11
  78.2 3.5 collective-permute-done.4
  81.8 4.0 collective-permute-start.5
  85.8 3.4 collective-permute-done.19
  89.3 2.0 collective-permute-start.20
  91.3 4.3 collective-permute-done.5
  95.7 2.1 collective-permute-start.6
  98.9 0.6 convolution_bitcast_fusion.4
  99.5 0.6 convolution_bitcast_fusion.5
  100.1 4.2 collective-permute-done.6
  105.0 0.6 convolution_bitcast_fusion.2
  105.6 0.6 convolution_bitcast_fusion.3
  106.4 1.1 fusion
  107.5 1.1 fusion.2
  109.6 0.6 fusion.46
  110.2 0.6 fusion.52
  111.1 0.6 fusion.4
  111.7 0.6 fusion.5
  112.4 0.6 copy-done.4
  114.1 0.7 fusion.7
  114.8 0.7 fusion.6
  115.6 0.9 convolution_bitcast_fusion.1
  116.5 0.6 convolution_bitcast_fusion
  118.9 2.2 collective-permute-start.21
  121.6 3.6 collective-permute-start.7
  125.2 4.2 collective-permute-done.7
  129.5 2.8 collective-permute-start.8
  132.5 3.9 collective-permute-start.22
  136.4 9.4 %collective-permute-done.8 = f32[2,16,2,512]{3,1,0,2:T(8,128)S(1)} collective-permute-done((f32[2,16,2,512]{3,1,0,2:T(8,128)S(1)}, f32[2,16,2,512]{3,1,0,2:T(8,128)S(1)}, u32[]{:S(2)}, u32[]{:S(2)}) %collective-permute-start.8) | collective-permute-done | bytes 131104 | tf_op jit(solution)/shard_map/ppermute | solution.py:11
  145.9 4.5 collective-permute-start.9
  150.6 5.6 collective-permute-start.23
  156.3 1.6 collective-permute-done.9
  157.9 7.1 %collective-permute-start.10 = (f32[2,16,2,512]{3,1,0,2:T(8,128)S(1)}, f32[2,16,2,512]{3,1,0,2:T(8,128)S(1)}, u32[]{:S(2)}, u32[]{:S(2)}) collective-permute-start(f32[2,16,2,512]{3,1,0,2:T(8,128)S(1)} %fusion.17), channel_id=1, source_target_pairs={{0,32},{4,36},{8,40},{12,44},{16,48},{20,52},{24,56},{28,60},{32,0... | collective-permute-start | bytes 393224 | tf_op jit(solution)/shard_map/ppermute | solution.py:11
  165.1 0.7 collective-permute-done.23
  165.9 3.3 collective-permute-start.24
  169.3 3.7 collective-permute-start.11
  173.6 3.3 collective-permute-start.25
  177.0 4.4 collective-permute-start.12
  181.9 4.4 collective-permute-start.26
  186.4 2.8 collective-permute-done.12
  189.2 4.3 collective-permute-start.13
  193.5 4.0 collective-permute-done.26
  197.6 4.7 collective-permute-start.27
  202.5 10.7 %collective-permute-done.27 = f32[2,17,2,512]{3,1,2,0:T(8,128)S(1)} collective-permute-done((f32[2,17,2,512]{3,1,2,0:T(8,128)S(1)}, f32[2,17,2,512]{3,1,2,0:T(8,128)S(1)}, u32[]{:S(2)}, u32[]{:S(2)}) %collective-permute-start.27) | collective-permute-done | bytes 139296 | tf_op jit(solution)/shard_map/ppermute | solution.py:11
  213.6 93.2 %all-reduce.3 = (f32[16]{0:T(128)S(1)}, f32[16]{0:T(128)S(1)}) all-reduce(f32[16]{0:T(128)S(1)} %get-tuple-element.8, f32[16]{0:T(128)S(1)} %mul.2458), channel_id=1, replica_groups=mesh['seq'=128,'ch'=4] {'seq','ch'}, use_global_device_ids=true, to_apply=%region_5.6 | all-reduce | flops 32 | bytes 256 | tf_op jit(solution)/shard_map/psum | solution.py:192
  307.9 0.8 fusion.29
  308.7 0.6 fusion.28
  309.3 306.7 %psum.21 = f32[16]{0:T(128)S(1)} all-reduce(f32[16]{0:T(128)S(1)} %get-tuple-element.130), channel_id=1, replica_groups=mesh['seq'=128,'ch'=4] {'seq'}, use_global_device_ids=true, to_apply=%region_3.4 | all-reduce | flops 16 | bytes 128 | tf_op jit(solution)/shard_map/psum | solution.py:193
  (195 shorter events, 12.9 us)
Async XLA Ops:
  0.8 0.7 copy-start.6
  0.8 0.7 copy-start.7
  1.4 0.7 copy-start.2
  1.5 0.7 copy-start.1
  2.3 7.8 %copy-start = (bf16[16,512]{1,0:T(8,128)(2,1)S(1)}, bf16[16,512]{1,0:T(8,128)(2,1)}, u32[]{:S(2)}) copy-start(bf16[16,512]{1,0:T(8,128)(2,1)} %param.9) | copy-start | bytes 49156
  2.3 7.8 %copy-start.3 = (bf16[16,512]{1,0:T(8,128)(2,1)S(1)}, bf16[16,512]{1,0:T(8,128)(2,1)}, u32[]{:S(2)}) copy-start(bf16[16,512]{1,0:T(8,128)(2,1)} %param.14) | copy-start | bytes 49156
  2.3 27.0 %collective-permute-start = (f32[2,17,2,512]{3,1,2,0:T(8,128)S(1)}, f32[2,17,2,512]{3,1,2,0:T(8,128)S(1)}, u32[]{:S(2)}, u32[]{:S(2)}) collective-permute-start(f32[2,17,2,512]{3,1,2,0:T(8,128)S(1)} %pad_maximum_fusion.13), channel_id=1, source_target_pairs={{0,256},{4,260},{8,264},{12,268},{16,272},{20,276},{24,280},{28,28... | collective-permute-start | bytes 417800 | tf_op jit(solution)/shard_map/ppermute | solution.py:11
  10.1 14.1 %collective-permute-start.14 = (f32[2,16,2,512]{3,1,0,2:T(8,128)S(1)}, f32[2,16,2,512]{3,1,0,2:T(8,128)S(1)}, u32[]{:S(2)}, u32[]{:S(2)}) collective-permute-start(f32[2,16,2,512]{3,1,0,2:T(8,128)S(1)} %pad_maximum_fusion.16), channel_id=1, source_target_pairs={{0,256},{4,260},{8,264},{12,268},{16,272},{20,276},{24,280},{28,28... | collective-permute-start | bytes 393224 | tf_op jit(solution)/shard_map/ppermute | solution.py:11
  24.4 14.9 %collective-permute-start.15 = (f32[2,16,2,512]{3,1,0,2:T(8,128)S(1)}, f32[2,16,2,512]{3,1,0,2:T(8,128)S(1)}, u32[]{:S(2)}, u32[]{:S(2)}) collective-permute-start(f32[2,16,2,512]{3,1,0,2:T(8,128)S(1)} %maximum_select_fusion.7), channel_id=1, source_target_pairs={{0,128},{4,132},{8,136},{12,140},{16,144},{20,148},{24,152},{28,15... | collective-permute-start | bytes 393224 | tf_op jit(solution)/shard_map/ppermute | solution.py:11
  29.4 13.7 %collective-permute-start.1 = (f32[2,17,2,512]{3,1,2,0:T(8,128)S(1)}, f32[2,17,2,512]{3,1,2,0:T(8,128)S(1)}, u32[]{:S(2)}, u32[]{:S(2)}) collective-permute-start(f32[2,17,2,512]{3,1,2,0:T(8,128)S(1)} %maximum_select_fusion), channel_id=1, source_target_pairs={{0,128},{4,132},{8,136},{12,140},{16,144},{20,148},{24,152},{28,15... | collective-permute-start | bytes 417800 | tf_op jit(solution)/shard_map/ppermute | solution.py:11
  39.4 6.9 %collective-permute-start.16 = (f32[2,16,2,512]{3,1,0,2:T(8,128)S(1)}, f32[2,16,2,512]{3,1,0,2:T(8,128)S(1)}, u32[]{:S(2)}, u32[]{:S(2)}) collective-permute-start(f32[2,16,2,512]{3,1,0,2:T(8,128)S(1)} %maximum_select_fusion.8), channel_id=1, source_target_pairs={{0,64},{4,68},{8,72},{12,76},{16,80},{20,84},{24,88},{28,92},{32,9... | collective-permute-start | bytes 393224 | tf_op jit(solution)/shard_map/ppermute | solution.py:11
  43.3 8.5 %collective-permute-start.2 = (f32[2,17,2,512]{3,1,2,0:T(8,128)S(1)}, f32[2,17,2,512]{3,1,2,0:T(8,128)S(1)}, u32[]{:S(2)}, u32[]{:S(2)}) collective-permute-start(f32[2,17,2,512]{3,1,2,0:T(8,128)S(1)} %maximum_select_fusion.1), channel_id=1, source_target_pairs={{0,64},{4,68},{8,72},{12,76},{16,80},{20,84},{24,88},{28,92},{32,9... | collective-permute-start | bytes 417800 | tf_op jit(solution)/shard_map/ppermute | solution.py:11
  46.3 8.7 %collective-permute-start.17 = (f32[2,16,2,512]{3,1,0,2:T(8,128)S(1)}, f32[2,16,2,512]{3,1,0,2:T(8,128)S(1)}, u32[]{:S(2)}, u32[]{:S(2)}) collective-permute-start(f32[2,16,2,512]{3,1,0,2:T(8,128)S(1)} %maximum_select_fusion.9), channel_id=1, source_target_pairs={{0,32},{4,36},{8,40},{12,44},{16,48},{20,52},{24,56},{28,60},{32,0... | collective-permute-start | bytes 393224 | tf_op jit(solution)/shard_map/ppermute | solution.py:11
  51.9 14.1 %collective-permute-start.3 = (f32[2,17,2,512]{3,1,2,0:T(8,128)S(1)}, f32[2,17,2,512]{3,1,2,0:T(8,128)S(1)}, u32[]{:S(2)}, u32[]{:S(2)}) collective-permute-start(f32[2,17,2,512]{3,1,2,0:T(8,128)S(1)} %maximum_select_fusion.2), channel_id=1, source_target_pairs={{0,32},{4,36},{8,40},{12,44},{16,48},{20,52},{24,56},{28,60},{32,0... | collective-permute-start | bytes 417800 | tf_op jit(solution)/shard_map/ppermute | solution.py:11
  55.1 15.6 %collective-permute-start.18 = (f32[2,16,2,512]{3,1,0,2:T(8,128)S(1)}, f32[2,16,2,512]{3,1,0,2:T(8,128)S(1)}, u32[]{:S(2)}, u32[]{:S(2)}) collective-permute-start(f32[2,16,2,512]{3,1,0,2:T(8,128)S(1)} %maximum_select_fusion.10), channel_id=1, source_target_pairs={{0,16},{4,20},{8,24},{12,28},{16,0},{20,4},{24,8},{28,12},{32,48},... | collective-permute-start | bytes 393224 | tf_op jit(solution)/shard_map/ppermute | solution.py:11
  66.2 15.5 %collective-permute-start.4 = (f32[2,17,2,512]{3,1,2,0:T(8,128)S(1)}, f32[2,17,2,512]{3,1,2,0:T(8,128)S(1)}, u32[]{:S(2)}, u32[]{:S(2)}) collective-permute-start(f32[2,17,2,512]{3,1,2,0:T(8,128)S(1)} %maximum_select_fusion.3), channel_id=1, source_target_pairs={{0,16},{4,20},{8,24},{12,28},{16,0},{20,4},{24,8},{28,12},{32,48},... | collective-permute-start | bytes 417800 | tf_op jit(solution)/shard_map/ppermute | solution.py:11
  70.8 18.4 %collective-permute-start.19 = (f32[2,16,2,512]{3,1,0,2:T(8,128)S(1)}, f32[2,16,2,512]{3,1,0,2:T(8,128)S(1)}, u32[]{:S(2)}, u32[]{:S(2)}) collective-permute-start(f32[2,16,2,512]{3,1,0,2:T(8,128)S(1)} %maximum_select_fusion.11), channel_id=1, source_target_pairs={{0,8},{4,12},{8,0},{12,4},{16,24},{20,28},{24,16},{28,20},{32,40},... | collective-permute-start | bytes 393224 | tf_op jit(solution)/shard_map/ppermute | solution.py:11
  81.8 13.8 %collective-permute-start.5 = (f32[2,17,2,512]{3,1,2,0:T(8,128)S(1)}, f32[2,17,2,512]{3,1,2,0:T(8,128)S(1)}, u32[]{:S(2)}, u32[]{:S(2)}) collective-permute-start(f32[2,17,2,512]{3,1,2,0:T(8,128)S(1)} %maximum_select_fusion.4), channel_id=1, source_target_pairs={{0,8},{4,12},{8,0},{12,4},{16,24},{20,28},{24,16},{28,20},{32,40},... | collective-permute-start | bytes 417800 | tf_op jit(solution)/shard_map/ppermute | solution.py:11
  89.3 8.9 %collective-permute-start.20 = (f32[2,16,2,512]{3,1,0,2:T(8,128)S(1)}, f32[2,16,2,512]{3,1,0,2:T(8,128)S(1)}, u32[]{:S(2)}, u32[]{:S(2)}) collective-permute-start(f32[2,16,2,512]{3,1,0,2:T(8,128)S(1)} %maximum_select_fusion.12), channel_id=1, source_target_pairs={{0,4},{4,0},{8,12},{12,8},{16,20},{20,16},{24,28},{28,24},{32,36},... | collective-permute-start | bytes 393224 | tf_op jit(solution)/shard_map/ppermute | solution.py:11
  95.7 8.6 %collective-permute-start.6 = (f32[2,17,2,512]{3,1,2,0:T(8,128)S(1)}, f32[2,17,2,512]{3,1,2,0:T(8,128)S(1)}, u32[]{:S(2)}, u32[]{:S(2)}) collective-permute-start(f32[2,17,2,512]{3,1,2,0:T(8,128)S(1)} %maximum_select_fusion.5), channel_id=1, source_target_pairs={{0,4},{4,0},{8,12},{12,8},{16,20},{20,16},{24,28},{28,24},{32,36},... | collective-permute-start | bytes 417800 | tf_op jit(solution)/shard_map/ppermute | solution.py:11
  112.4 0.7 copy-start.4
  118.9 13.5 %collective-permute-start.21 = (f32[2,17,2,512]{3,1,2,0:T(8,128)S(1)}, f32[2,17,2,512]{3,1,2,0:T(8,128)S(1)}, u32[]{:S(2)}, u32[]{:S(2)}) collective-permute-start(f32[2,17,2,512]{3,1,2,0:T(8,128)S(1)} %pad_maximum_fusion.14), channel_id=1, source_target_pairs={{0,4},{4,0},{8,12},{12,8},{16,20},{20,16},{24,28},{28,24},{32,36},... | collective-permute-start | bytes 417800 | tf_op jit(solution)/shard_map/ppermute | solution.py:11
  121.6 7.9 %collective-permute-start.7 = (f32[2,16,2,512]{3,1,0,2:T(8,128)S(1)}, f32[2,16,2,512]{3,1,0,2:T(8,128)S(1)}, u32[]{:S(2)}, u32[]{:S(2)}) collective-permute-start(f32[2,16,2,512]{3,1,0,2:T(8,128)S(1)} %pad_maximum_fusion.15), channel_id=1, source_target_pairs={{0,4},{4,0},{8,12},{12,8},{16,20},{20,16},{24,28},{28,24},{32,36},... | collective-permute-start | bytes 393224 | tf_op jit(solution)/shard_map/ppermute | solution.py:11
  129.5 16.3 %collective-permute-start.8 = (f32[2,16,2,512]{3,1,0,2:T(8,128)S(1)}, f32[2,16,2,512]{3,1,0,2:T(8,128)S(1)}, u32[]{:S(2)}, u32[]{:S(2)}) collective-permute-start(f32[2,16,2,512]{3,1,0,2:T(8,128)S(1)} %fusion.15), channel_id=1, source_target_pairs={{0,8},{4,12},{8,0},{12,4},{16,24},{20,28},{24,16},{28,20},{32,40},... | collective-permute-start | bytes 393224 | tf_op jit(solution)/shard_map/ppermute | solution.py:11
  132.5 17.9 %collective-permute-start.22 = (f32[2,17,2,512]{3,1,2,0:T(8,128)S(1)}, f32[2,17,2,512]{3,1,2,0:T(8,128)S(1)}, u32[]{:S(2)}, u32[]{:S(2)}) collective-permute-start(f32[2,17,2,512]{3,1,2,0:T(8,128)S(1)} %fusion.8), channel_id=1, source_target_pairs={{0,8},{4,12},{8,0},{12,4},{16,24},{20,28},{24,16},{28,20},{32,40},... | collective-permute-start | bytes 417800 | tf_op jit(solution)/shard_map/ppermute | solution.py:11
  145.9 11.9 %collective-permute-start.9 = (f32[2,16,2,512]{3,1,0,2:T(8,128)S(1)}, f32[2,16,2,512]{3,1,0,2:T(8,128)S(1)}, u32[]{:S(2)}, u32[]{:S(2)}) collective-permute-start(f32[2,16,2,512]{3,1,0,2:T(8,128)S(1)} %fusion.16), channel_id=1, source_target_pairs={{0,16},{4,20},{8,24},{12,28},{16,0},{20,4},{24,8},{28,12},{32,48},... | collective-permute-start | bytes 393224 | tf_op jit(solution)/shard_map/ppermute | solution.py:11
  150.6 15.2 %collective-permute-start.23 = (f32[2,17,2,512]{3,1,2,0:T(8,128)S(1)}, f32[2,17,2,512]{3,1,2,0:T(8,128)S(1)}, u32[]{:S(2)}, u32[]{:S(2)}) collective-permute-start(f32[2,17,2,512]{3,1,2,0:T(8,128)S(1)} %fusion.9), channel_id=1, source_target_pairs={{0,16},{4,20},{8,24},{12,28},{16,0},{20,4},{24,8},{28,12},{32,48},... | collective-permute-start | bytes 417800 | tf_op jit(solution)/shard_map/ppermute | solution.py:11
  157.9 11.3 %collective-permute-start.10 = (f32[2,16,2,512]{3,1,0,2:T(8,128)S(1)}, f32[2,16,2,512]{3,1,0,2:T(8,128)S(1)}, u32[]{:S(2)}, u32[]{:S(2)}) collective-permute-start(f32[2,16,2,512]{3,1,0,2:T(8,128)S(1)} %fusion.17), channel_id=1, source_target_pairs={{0,32},{4,36},{8,40},{12,44},{16,48},{20,52},{24,56},{28,60},{32,0... | collective-permute-start | bytes 393224 | tf_op jit(solution)/shard_map/ppermute | solution.py:11
  165.9 7.6 %collective-permute-start.24 = (f32[2,17,2,512]{3,1,2,0:T(8,128)S(1)}, f32[2,17,2,512]{3,1,2,0:T(8,128)S(1)}, u32[]{:S(2)}, u32[]{:S(2)}) collective-permute-start(f32[2,17,2,512]{3,1,2,0:T(8,128)S(1)} %fusion.10), channel_id=1, source_target_pairs={{0,32},{4,36},{8,40},{12,44},{16,48},{20,52},{24,56},{28,60},{32,0... | collective-permute-start | bytes 417800 | tf_op jit(solution)/shard_map/ppermute | solution.py:11
  169.3 7.6 %collective-permute-start.11 = (f32[2,16,2,512]{3,1,0,2:T(8,128)S(1)}, f32[2,16,2,512]{3,1,0,2:T(8,128)S(1)}, u32[]{:S(2)}, u32[]{:S(2)}) collective-permute-start(f32[2,16,2,512]{3,1,0,2:T(8,128)S(1)} %fusion.18), channel_id=1, source_target_pairs={{0,64},{4,68},{8,72},{12,76},{16,80},{20,84},{24,88},{28,92},{32,9... | collective-permute-start | bytes 393224 | tf_op jit(solution)/shard_map/ppermute | solution.py:11
  173.6 8.2 %collective-permute-start.25 = (f32[2,17,2,512]{3,1,2,0:T(8,128)S(1)}, f32[2,17,2,512]{3,1,2,0:T(8,128)S(1)}, u32[]{:S(2)}, u32[]{:S(2)}) collective-permute-start(f32[2,17,2,512]{3,1,2,0:T(8,128)S(1)} %fusion.11), channel_id=1, source_target_pairs={{0,64},{4,68},{8,72},{12,76},{16,80},{20,84},{24,88},{28,92},{32,9... | collective-permute-start | bytes 417800 | tf_op jit(solution)/shard_map/ppermute | solution.py:11
  177.0 12.1 %collective-permute-start.12 = (f32[2,16,2,512]{3,1,0,2:T(8,128)S(1)}, f32[2,16,2,512]{3,1,0,2:T(8,128)S(1)}, u32[]{:S(2)}, u32[]{:S(2)}) collective-permute-start(f32[2,16,2,512]{3,1,0,2:T(8,128)S(1)} %fusion.19), channel_id=1, source_target_pairs={{0,128},{4,132},{8,136},{12,140},{16,144},{20,148},{24,152},{28,15... | collective-permute-start | bytes 393224 | tf_op jit(solution)/shard_map/ppermute | solution.py:11
  181.9 15.6 %collective-permute-start.26 = (f32[2,17,2,512]{3,1,2,0:T(8,128)S(1)}, f32[2,17,2,512]{3,1,2,0:T(8,128)S(1)}, u32[]{:S(2)}, u32[]{:S(2)}) collective-permute-start(f32[2,17,2,512]{3,1,2,0:T(8,128)S(1)} %fusion.12), channel_id=1, source_target_pairs={{0,128},{4,132},{8,136},{12,140},{16,144},{20,148},{24,152},{28,15... | collective-permute-start | bytes 417800 | tf_op jit(solution)/shard_map/ppermute | solution.py:11
  189.2 13.1 %collective-permute-start.13 = (f32[2,16,2,512]{3,1,0,2:T(8,128)S(1)}, f32[2,16,2,512]{3,1,0,2:T(8,128)S(1)}, u32[]{:S(2)}, u32[]{:S(2)}) collective-permute-start(f32[2,16,2,512]{3,1,0,2:T(8,128)S(1)} %fusion.20), channel_id=1, source_target_pairs={{0,256},{4,260},{8,264},{12,268},{16,272},{20,276},{24,280},{28,28... | collective-permute-start | bytes 393224 | tf_op jit(solution)/shard_map/ppermute | solution.py:11
  197.6 15.6 %collective-permute-start.27 = (f32[2,17,2,512]{3,1,2,0:T(8,128)S(1)}, f32[2,17,2,512]{3,1,2,0:T(8,128)S(1)}, u32[]{:S(2)}, u32[]{:S(2)}) collective-permute-start(f32[2,17,2,512]{3,1,2,0:T(8,128)S(1)} %fusion.13), channel_id=1, source_target_pairs={{0,256},{4,260},{8,264},{12,268},{16,272},{20,276},{24,280},{28,28... | collective-permute-start | bytes 417800 | tf_op jit(solution)/shard_map/ppermute | solution.py:11
  307.3 0.7 copy-start.5
where the time goes:
time: 618 us; the launch traced here: 617 us
  blocking collectives  400 us (65%)
  starting transfers between devices  115 us (19%)
  waiting for transfers between devices  73.9 us (12%)
  matrix products  11.2 us (2%)
  other arithmetic  7.95 us (1%)
    psum x1, blocking collectives, per_device(): sum_skip = lax.psum(part_skip, 'seq')  307 us
    ppermute x28, starting transfers between devices, partner_2(): lax.ppermute(shard, axis, [(i, i ^ 1 << stride) for i in range(lax.axis_s...  115 us
    psum x1, blocking collectives, per_device(): lax.psum((part_residue, part_memory), ('seq', 'ch'))  93.2 us
    ppermute x28, waiting for transfers between devices, partner_2(): lax.ppermute(shard, axis, [(i, i ^ 1 << stride) for i in range(lax.axis_s...  73.9 us
  transfers between devices with their start and end apart: 28, of which 20 were waited for; matrix products, arithmetic and copies ran while one was open for 1% of the time, Pallas kernels for 0%

commit v1 on v0

--- a/solution.py
+++ b/solution.py
@@ -3,8 +3,13 @@
 import jax.numpy as jnp
 from jax import lax
 from jax.sharding import PartitionSpec as P
+from jax.lax import psum
 
 HIGH_PREC = lax.Precision.HIGHEST
+
+
+def register_steps_all(x_in, chip_axis, net_axis="seq"):
+    return psum(psum(x_in, chip_axis), net_axis)
 
 
 def partner_2(shard, axis, stride):
@@ -189,7 +194,7 @@
     part_skip = jnp.sum(grad_mixed * values, axis=1)
     all_channels = channels * lax.axis_size("ch")
     seq_total = devices * local_len
-    sum_residue, sum_memory = lax.psum((part_residue, part_memory), ("seq", "ch"))
+    sum_residue, sum_memory = register_steps_all((part_residue, part_memory), "ch")
     sum_skip = lax.psum(part_skip, "seq")
     norm_scale = 1.0 / math.sqrt(all_channels * seq_total)
     grad_skip = sum_skip / math.sqrt(seq_total)

time: 618 us -> 531 us (0.86)
  blocking collectives: 400 us -> 314 us
    psum x1, blocking collectives: 93.2 us -> 7.27 us  [register_steps_all(): return psum(psum(x_in, chip_axis), net_axis)]
where the time goes in v1:
time: 531 us; the launch traced here: 530 us
  blocking collectives  314 us (59%)
  starting transfers between devices  115 us (22%)
  waiting for transfers between devices  73.9 us (14%)
  matrix products  11.2 us (2%)
  other arithmetic  7.94 us (1%)
    psum x1, blocking collectives, per_device(): sum_skip = lax.psum(part_skip, 'seq')  306 us
    ppermute x28, starting transfers between devices, partner_2(): lax.ppermute(shard, axis, [(i, i ^ 1 << stride) for i in range(lax.axis_s...  115 us
    ppermute x28, waiting for transfers between devices, partner_2(): lax.ppermute(shard, axis, [(i, i ^ 1 << stride) for i in range(lax.axis_s...  73.9 us
  transfers between devices with their start and end apart: 28, of which 20 were waited for; matrix products, arithmetic and copies ran while one was open for 1% of the time, Pallas kernels for 0%

profile of v1, /device:TPU:4, one launch (start us, length us, event | category | flops | bytes accessed | tf_op | source)
XLA Modules:
  0.0 530.1 jit_solution(325985558130426324)
XLA Ops:
  0.8 0.6 copy-done.6
  2.3 7.7 %collective-permute-start = (f32[2,17,2,512]{3,1,2,0:T(8,128)S(1)}, f32[2,17,2,512]{3,1,2,0:T(8,128)S(1)}, u32[]{:S(2)}, u32[]{:S(2)}) collective-permute-start(f32[2,17,2,512]{3,1,2,0:T(8,128)S(1)} %pad_maximum_fusion.13), channel_id=1, source_target_pairs={{0,256},{4,260},{8,264},{12,268},{16,272},{20,276},{24,280},{28,28... | collective-permute-start | bytes 417800 | tf_op jit(solution)/shard_map/ppermute | solution.py:16
  10.1 2.0 collective-permute-start.14
  13.4 10.8 %collective-permute-done.14 = f32[2,16,2,512]{3,1,0,2:T(8,128)S(1)} collective-permute-done((f32[2,16,2,512]{3,1,0,2:T(8,128)S(1)}, f32[2,16,2,512]{3,1,0,2:T(8,128)S(1)}, u32[]{:S(2)}, u32[]{:S(2)}) %collective-permute-start.14) | collective-permute-done | bytes 131104 | tf_op jit(solution)/shard_map/ppermute | solution.py:16
  24.4 4.9 collective-permute-start.15
  29.4 1.9 collective-permute-start.1
  31.4 7.9 %collective-permute-done.15 = f32[2,16,2,512]{3,1,0,2:T(8,128)S(1)} collective-permute-done((f32[2,16,2,512]{3,1,0,2:T(8,128)S(1)}, f32[2,16,2,512]{3,1,0,2:T(8,128)S(1)}, u32[]{:S(2)}, u32[]{:S(2)}) %collective-permute-start.15) | collective-permute-done | bytes 131104 | tf_op jit(solution)/shard_map/ppermute | solution.py:16
  39.4 1.9 collective-permute-start.16
  41.3 1.8 collective-permute-done.1
  43.3 2.1 collective-permute-start.2
  45.5 0.8 collective-permute-done.16
  46.3 3.1 collective-permute-start.17
  49.4 2.4 collective-permute-done.2
  51.9 3.1 collective-permute-start.3
  55.1 10.9 %collective-permute-start.18 = (f32[2,16,2,512]{3,1,0,2:T(8,128)S(1)}, f32[2,16,2,512]{3,1,0,2:T(8,128)S(1)}, u32[]{:S(2)}, u32[]{:S(2)}) collective-permute-start(f32[2,16,2,512]{3,1,0,2:T(8,128)S(1)} %maximum_select_fusion.10), channel_id=1, source_target_pairs={{0,16},{4,20},{8,24},{12,28},{16,0},{20,4},{24,8},{28,12},{32,48},... | collective-permute-start | bytes 393224 | tf_op jit(solution)/shard_map/ppermute | solution.py:16
  66.2 4.3 collective-permute-start.4
  70.8 7.4 %collective-permute-start.19 = (f32[2,16,2,512]{3,1,0,2:T(8,128)S(1)}, f32[2,16,2,512]{3,1,0,2:T(8,128)S(1)}, u32[]{:S(2)}, u32[]{:S(2)}) collective-permute-start(f32[2,16,2,512]{3,1,0,2:T(8,128)S(1)} %maximum_select_fusion.11), channel_id=1, source_target_pairs={{0,8},{4,12},{8,0},{12,4},{16,24},{20,28},{24,16},{28,20},{32,40},... | collective-permute-start | bytes 393224 | tf_op jit(solution)/shard_map/ppermute | solution.py:16
  78.2 3.5 collective-permute-done.4
  81.8 4.0 collective-permute-start.5
  85.8 3.4 collective-permute-done.19
  89.3 2.0 collective-permute-start.20
  91.3 4.3 collective-permute-done.5
  95.7 2.1 collective-permute-start.6
  98.9 0.6 convolution_bitcast_fusion.4
  99.5 0.6 convolution_bitcast_fusion.5
  100.1 4.2 collective-permute-done.6
  105.0 0.6 convolution_bitcast_fusion.2
  105.6 0.6 convolution_bitcast_fusion.3
  106.4 1.1 fusion
  107.5 1.1 fusion.2
  109.6 0.6 fusion.46
  110.2 0.6 fusion.52
  111.1 0.6 fusion.4
  111.7 0.6 fusion.5
  112.4 0.6 copy-done.4
  114.1 0.7 fusion.7
  114.8 0.7 fusion.6
  115.6 0.9 convolution_bitcast_fusion.1
  116.5 0.6 convolution_bitcast_fusion
  118.9 2.2 collective-permute-start.21
  121.6 3.6 collective-permute-start.7
  125.2 4.2 collective-permute-done.7
  129.5 2.8 collective-permute-start.8
  132.5 3.9 collective-permute-start.22
  136.4 9.4 %collective-permute-done.8 = f32[2,16,2,512]{3,1,0,2:T(8,128)S(1)} collective-permute-done((f32[2,16,2,512]{3,1,0,2:T(8,128)S(1)}, f32[2,16,2,512]{3,1,0,2:T(8,128)S(1)}, u32[]{:S(2)}, u32[]{:S(2)}) %collective-permute-start.8) | collective-permute-done | bytes 131104 | tf_op jit(solution)/shard_map/ppermute | solution.py:16
  145.9 4.5 collective-permute-start.9
  150.6 5.6 %collective-permute-start.23 = (f32[2,17,2,512]{3,1,2,0:T(8,128)S(1)}, f32[2,17,2,512]{3,1,2,0:T(8,128)S(1)}, u32[]{:S(2)}, u32[]{:S(2)}) collective-permute-start(f32[2,17,2,512]{3,1,2,0:T(8,128)S(1)} %fusion.9), channel_id=1, source_target_pairs={{0,16},{4,20},{8,24},{12,28},{16,0},{20,4},{24,8},{28,12},{32,48},... | collective-permute-start | bytes 417800 | tf_op jit(solution)/shard_map/ppermute | solution.py:16
  156.3 1.6 collective-permute-done.9
  157.9 7.1 %collective-permute-start.10 = (f32[2,16,2,512]{3,1,0,2:T(8,128)S(1)}, f32[2,16,2,512]{3,1,0,2:T(8,128)S(1)}, u32[]{:S(2)}, u32[]{:S(2)}) collective-permute-start(f32[2,16,2,512]{3,1,0,2:T(8,128)S(1)} %fusion.17), channel_id=1, source_target_pairs={{0,32},{4,36},{8,40},{12,44},{16,48},{20,52},{24,56},{28,60},{32,0... | collective-permute-start | bytes 393224 | tf_op jit(solution)/shard_map/ppermute | solution.py:16
  165.1 0.7 collective-permute-done.23
  165.9 3.3 collective-permute-start.24
  169.3 3.7 collective-permute-start.11
  173.6 3.3 collective-permute-start.25
  177.0 4.4 collective-permute-start.12
  181.9 4.4 collective-permute-start.26
  186.4 2.8 collective-permute-done.12
  189.2 4.3 collective-permute-start.13
  193.5 4.0 collective-permute-done.26
  197.6 4.7 collective-permute-start.27
  202.5 10.7 %collective-permute-done.27 = f32[2,17,2,512]{3,1,2,0:T(8,128)S(1)} collective-permute-done((f32[2,17,2,512]{3,1,2,0:T(8,128)S(1)}, f32[2,17,2,512]{3,1,2,0:T(8,128)S(1)}, u32[]{:S(2)}, u32[]{:S(2)}) %collective-permute-start.27) | collective-permute-done | bytes 139296 | tf_op jit(solution)/shard_map/ppermute | solution.py:16
  213.6 7.3 %all-reduce.4 = (f32[16]{0:T(128)S(1)}, f32[16]{0:T(128)S(1)}) all-reduce(f32[16]{0:T(128)S(1)} %get-tuple-element.8, f32[16]{0:T(128)S(1)} %mul.2458), channel_id=1, replica_groups=mesh['seq'=128,'ch'=4] {'ch'}, use_global_device_ids=true, to_apply=%region_5.6 | all-reduce | flops 32 | bytes 256 | tf_op jit(solution)/shard_map/psum | solution.py:12
  220.9 0.8 fusion.29
  221.7 306.3 %all-reduce.3 = (f32[16]{0:T(128)S(1)}, f32[16]{0:T(128)S(1)}, f32[16]{0:T(128)S(1)}) all-reduce(f32[16]{0:T(128)S(1)} %get-tuple-element.133, f32[16]{0:T(128)S(1)} %get-tuple-element.12, f32[16]{0:T(128)S(1)} %get-tuple-element.13), channel_id=1, replica_groups=mesh['seq'=128,'ch'=4] {'seq'}, use_global_device_ids=true, to_apply=%region_3.4 | all-reduce | flops 48 | bytes 384 | tf_op jit(solution)/shard_map/psum | solution.py:198
  529.5 0.6 fusion.28
  (195 shorter events, 12.8 us)
Async XLA Ops:
  0.8 0.7 copy-start.6
  0.8 0.7 copy-start.7
  1.4 0.7 copy-start.2
  1.5 0.7 copy-start.1
  2.3 7.8 %copy-start = (bf16[16,512]{1,0:T(8,128)(2,1)S(1)}, bf16[16,512]{1,0:T(8,128)(2,1)}, u32[]{:S(2)}) copy-start(bf16[16,512]{1,0:T(8,128)(2,1)} %param.9) | copy-start | bytes 49156
  2.3 7.8 %copy-start.3 = (bf16[16,512]{1,0:T(8,128)(2,1)S(1)}, bf16[16,512]{1,0:T(8,128)(2,1)}, u32[]{:S(2)}) copy-start(bf16[16,512]{1,0:T(8,128)(2,1)} %param.14) | copy-start | bytes 49156
  2.3 27.0 %collective-permute-start = (f32[2,17,2,512]{3,1,2,0:T(8,128)S(1)}, f32[2,17,2,512]{3,1,2,0:T(8,128)S(1)}, u32[]{:S(2)}, u32[]{:S(2)}) collective-permute-start(f32[2,17,2,512]{3,1,2,0:T(8,128)S(1)} %pad_maximum_fusion.13), channel_id=1, source_target_pairs={{0,256},{4,260},{8,264},{12,268},{16,272},{20,276},{24,280},{28,28... | collective-permute-start | bytes 417800 | tf_op jit(solution)/shard_map/ppermute | solution.py:16
  10.1 14.1 %collective-permute-start.14 = (f32[2,16,2,512]{3,1,0,2:T(8,128)S(1)}, f32[2,16,2,512]{3,1,0,2:T(8,128)S(1)}, u32[]{:S(2)}, u32[]{:S(2)}) collective-permute-start(f32[2,16,2,512]{3,1,0,2:T(8,128)S(1)} %pad_maximum_fusion.16), channel_id=1, source_target_pairs={{0,256},{4,260},{8,264},{12,268},{16,272},{20,276},{24,280},{28,28... | collective-permute-start | bytes 393224 | tf_op jit(solution)/shard_map/ppermute | solution.py:16
  24.4 14.9 %collective-permute-start.15 = (f32[2,16,2,512]{3,1,0,2:T(8,128)S(1)}, f32[2,16,2,512]{3,1,0,2:T(8,128)S(1)}, u32[]{:S(2)}, u32[]{:S(2)}) collective-permute-start(f32[2,16,2,512]{3,1,0,2:T(8,128)S(1)} %maximum_select_fusion.7), channel_id=1, source_target_pairs={{0,128},{4,132},{8,136},{12,140},{16,144},{20,148},{24,152},{28,15... | collective-permute-start | bytes 393224 | tf_op jit(solution)/shard_map/ppermute | solution.py:16
  29.4 13.7 %collective-permute-start.1 = (f32[2,17,2,512]{3,1,2,0:T(8,128)S(1)}, f32[2,17,2,512]{3,1,2,0:T(8,128)S(1)}, u32[]{:S(2)}, u32[]{:S(2)}) collective-permute-start(f32[2,17,2,512]{3,1,2,0:T(8,128)S(1)} %maximum_select_fusion), channel_id=1, source_target_pairs={{0,128},{4,132},{8,136},{12,140},{16,144},{20,148},{24,152},{28,15... | collective-permute-start | bytes 417800 | tf_op jit(solution)/shard_map/ppermute | solution.py:16
  39.4 6.9 %collective-permute-start.16 = (f32[2,16,2,512]{3,1,0,2:T(8,128)S(1)}, f32[2,16,2,512]{3,1,0,2:T(8,128)S(1)}, u32[]{:S(2)}, u32[]{:S(2)}) collective-permute-start(f32[2,16,2,512]{3,1,0,2:T(8,128)S(1)} %maximum_select_fusion.8), channel_id=1, source_target_pairs={{0,64},{4,68},{8,72},{12,76},{16,80},{20,84},{24,88},{28,92},{32,9... | collective-permute-start | bytes 393224 | tf_op jit(solution)/shard_map/ppermute | solution.py:16
  43.3 8.5 %collective-permute-start.2 = (f32[2,17,2,512]{3,1,2,0:T(8,128)S(1)}, f32[2,17,2,512]{3,1,2,0:T(8,128)S(1)}, u32[]{:S(2)}, u32[]{:S(2)}) collective-permute-start(f32[2,17,2,512]{3,1,2,0:T(8,128)S(1)} %maximum_select_fusion.1), channel_id=1, source_target_pairs={{0,64},{4,68},{8,72},{12,76},{16,80},{20,84},{24,88},{28,92},{32,9... | collective-permute-start | bytes 417800 | tf_op jit(solution)/shard_map/ppermute | solution.py:16
  46.3 8.7 %collective-permute-start.17 = (f32[2,16,2,512]{3,1,0,2:T(8,128)S(1)}, f32[2,16,2,512]{3,1,0,2:T(8,128)S(1)}, u32[]{:S(2)}, u32[]{:S(2)}) collective-permute-start(f32[2,16,2,512]{3,1,0,2:T(8,128)S(1)} %maximum_select_fusion.9), channel_id=1, source_target_pairs={{0,32},{4,36},{8,40},{12,44},{16,48},{20,52},{24,56},{28,60},{32,0... | collective-permute-start | bytes 393224 | tf_op jit(solution)/shard_map/ppermute | solution.py:16
  51.9 14.1 %collective-permute-start.3 = (f32[2,17,2,512]{3,1,2,0:T(8,128)S(1)}, f32[2,17,2,512]{3,1,2,0:T(8,128)S(1)}, u32[]{:S(2)}, u32[]{:S(2)}) collective-permute-start(f32[2,17,2,512]{3,1,2,0:T(8,128)S(1)} %maximum_select_fusion.2), channel_id=1, source_target_pairs={{0,32},{4,36},{8,40},{12,44},{16,48},{20,52},{24,56},{28,60},{32,0... | collective-permute-start | bytes 417800 | tf_op jit(solution)/shard_map/ppermute | solution.py:16
  55.1 15.6 %collective-permute-start.18 = (f32[2,16,2,512]{3,1,0,2:T(8,128)S(1)}, f32[2,16,2,512]{3,1,0,2:T(8,128)S(1)}, u32[]{:S(2)}, u32[]{:S(2)}) collective-permute-start(f32[2,16,2,512]{3,1,0,2:T(8,128)S(1)} %maximum_select_fusion.10), channel_id=1, source_target_pairs={{0,16},{4,20},{8,24},{12,28},{16,0},{20,4},{24,8},{28,12},{32,48},... | collective-permute-start | bytes 393224 | tf_op jit(solution)/shard_map/ppermute | solution.py:16
  66.2 15.5 %collective-permute-start.4 = (f32[2,17,2,512]{3,1,2,0:T(8,128)S(1)}, f32[2,17,2,512]{3,1,2,0:T(8,128)S(1)}, u32[]{:S(2)}, u32[]{:S(2)}) collective-permute-start(f32[2,17,2,512]{3,1,2,0:T(8,128)S(1)} %maximum_select_fusion.3), channel_id=1, source_target_pairs={{0,16},{4,20},{8,24},{12,28},{16,0},{20,4},{24,8},{28,12},{32,48},... | collective-permute-start | bytes 417800 | tf_op jit(solution)/shard_map/ppermute | solution.py:16
  70.8 18.4 %collective-permute-start.19 = (f32[2,16,2,512]{3,1,0,2:T(8,128)S(1)}, f32[2,16,2,512]{3,1,0,2:T(8,128)S(1)}, u32[]{:S(2)}, u32[]{:S(2)}) collective-permute-start(f32[2,16,2,512]{3,1,0,2:T(8,128)S(1)} %maximum_select_fusion.11), channel_id=1, source_target_pairs={{0,8},{4,12},{8,0},{12,4},{16,24},{20,28},{24,16},{28,20},{32,40},... | collective-permute-start | bytes 393224 | tf_op jit(solution)/shard_map/ppermute | solution.py:16
  81.8 13.8 %collective-permute-start.5 = (f32[2,17,2,512]{3,1,2,0:T(8,128)S(1)}, f32[2,17,2,512]{3,1,2,0:T(8,128)S(1)}, u32[]{:S(2)}, u32[]{:S(2)}) collective-permute-start(f32[2,17,2,512]{3,1,2,0:T(8,128)S(1)} %maximum_select_fusion.4), channel_id=1, source_target_pairs={{0,8},{4,12},{8,0},{12,4},{16,24},{20,28},{24,16},{28,20},{32,40},... | collective-permute-start | bytes 417800 | tf_op jit(solution)/shard_map/ppermute | solution.py:16
  89.3 8.9 %collective-permute-start.20 = (f32[2,16,2,512]{3,1,0,2:T(8,128)S(1)}, f32[2,16,2,512]{3,1,0,2:T(8,128)S(1)}, u32[]{:S(2)}, u32[]{:S(2)}) collective-permute-start(f32[2,16,2,512]{3,1,0,2:T(8,128)S(1)} %maximum_select_fusion.12), channel_id=1, source_target_pairs={{0,4},{4,0},{8,12},{12,8},{16,20},{20,16},{24,28},{28,24},{32,36},... | collective-permute-start | bytes 393224 | tf_op jit(solution)/shard_map/ppermute | solution.py:16
  95.7 8.6 %collective-permute-start.6 = (f32[2,17,2,512]{3,1,2,0:T(8,128)S(1)}, f32[2,17,2,512]{3,1,2,0:T(8,128)S(1)}, u32[]{:S(2)}, u32[]{:S(2)}) collective-permute-start(f32[2,17,2,512]{3,1,2,0:T(8,128)S(1)} %maximum_select_fusion.5), channel_id=1, source_target_pairs={{0,4},{4,0},{8,12},{12,8},{16,20},{20,16},{24,28},{28,24},{32,36},... | collective-permute-start | bytes 417800 | tf_op jit(solution)/shard_map/ppermute | solution.py:16
  112.4 0.7 copy-start.4
  118.9 13.5 %collective-permute-start.21 = (f32[2,17,2,512]{3,1,2,0:T(8,128)S(1)}, f32[2,17,2,512]{3,1,2,0:T(8,128)S(1)}, u32[]{:S(2)}, u32[]{:S(2)}) collective-permute-start(f32[2,17,2,512]{3,1,2,0:T(8,128)S(1)} %pad_maximum_fusion.14), channel_id=1, source_target_pairs={{0,4},{4,0},{8,12},{12,8},{16,20},{20,16},{24,28},{28,24},{32,36},... | collective-permute-start | bytes 417800 | tf_op jit(solution)/shard_map/ppermute | solution.py:16
  121.6 7.9 %collective-permute-start.7 = (f32[2,16,2,512]{3,1,0,2:T(8,128)S(1)}, f32[2,16,2,512]{3,1,0,2:T(8,128)S(1)}, u32[]{:S(2)}, u32[]{:S(2)}) collective-permute-start(f32[2,16,2,512]{3,1,0,2:T(8,128)S(1)} %pad_maximum_fusion.15), channel_id=1, source_target_pairs={{0,4},{4,0},{8,12},{12,8},{16,20},{20,16},{24,28},{28,24},{32,36},... | collective-permute-start | bytes 393224 | tf_op jit(solution)/shard_map/ppermute | solution.py:16
  129.5 16.3 %collective-permute-start.8 = (f32[2,16,2,512]{3,1,0,2:T(8,128)S(1)}, f32[2,16,2,512]{3,1,0,2:T(8,128)S(1)}, u32[]{:S(2)}, u32[]{:S(2)}) collective-permute-start(f32[2,16,2,512]{3,1,0,2:T(8,128)S(1)} %fusion.15), channel_id=1, source_target_pairs={{0,8},{4,12},{8,0},{12,4},{16,24},{20,28},{24,16},{28,20},{32,40},... | collective-permute-start | bytes 393224 | tf_op jit(solution)/shard_map/ppermute | solution.py:16
  132.5 17.9 %collective-permute-start.22 = (f32[2,17,2,512]{3,1,2,0:T(8,128)S(1)}, f32[2,17,2,512]{3,1,2,0:T(8,128)S(1)}, u32[]{:S(2)}, u32[]{:S(2)}) collective-permute-start(f32[2,17,2,512]{3,1,2,0:T(8,128)S(1)} %fusion.8), channel_id=1, source_target_pairs={{0,8},{4,12},{8,0},{12,4},{16,24},{20,28},{24,16},{28,20},{32,40},... | collective-permute-start | bytes 417800 | tf_op jit(solution)/shard_map/ppermute | solution.py:16
  145.9 11.9 %collective-permute-start.9 = (f32[2,16,2,512]{3,1,0,2:T(8,128)S(1)}, f32[2,16,2,512]{3,1,0,2:T(8,128)S(1)}, u32[]{:S(2)}, u32[]{:S(2)}) collective-permute-start(f32[2,16,2,512]{3,1,0,2:T(8,128)S(1)} %fusion.16), channel_id=1, source_target_pairs={{0,16},{4,20},{8,24},{12,28},{16,0},{20,4},{24,8},{28,12},{32,48},... | collective-permute-start | bytes 393224 | tf_op jit(solution)/shard_map/ppermute | solution.py:16
  150.6 15.2 %collective-permute-start.23 = (f32[2,17,2,512]{3,1,2,0:T(8,128)S(1)}, f32[2,17,2,512]{3,1,2,0:T(8,128)S(1)}, u32[]{:S(2)}, u32[]{:S(2)}) collective-permute-start(f32[2,17,2,512]{3,1,2,0:T(8,128)S(1)} %fusion.9), channel_id=1, source_target_pairs={{0,16},{4,20},{8,24},{12,28},{16,0},{20,4},{24,8},{28,12},{32,48},... | collective-permute-start | bytes 417800 | tf_op jit(solution)/shard_map/ppermute | solution.py:16
  157.9 11.3 %collective-permute-start.10 = (f32[2,16,2,512]{3,1,0,2:T(8,128)S(1)}, f32[2,16,2,512]{3,1,0,2:T(8,128)S(1)}, u32[]{:S(2)}, u32[]{:S(2)}) collective-permute-start(f32[2,16,2,512]{3,1,0,2:T(8,128)S(1)} %fusion.17), channel_id=1, source_target_pairs={{0,32},{4,36},{8,40},{12,44},{16,48},{20,52},{24,56},{28,60},{32,0... | collective-permute-start | bytes 393224 | tf_op jit(solution)/shard_map/ppermute | solution.py:16
  165.9 7.6 %collective-permute-start.24 = (f32[2,17,2,512]{3,1,2,0:T(8,128)S(1)}, f32[2,17,2,512]{3,1,2,0:T(8,128)S(1)}, u32[]{:S(2)}, u32[]{:S(2)}) collective-permute-start(f32[2,17,2,512]{3,1,2,0:T(8,128)S(1)} %fusion.10), channel_id=1, source_target_pairs={{0,32},{4,36},{8,40},{12,44},{16,48},{20,52},{24,56},{28,60},{32,0... | collective-permute-start | bytes 417800 | tf_op jit(solution)/shard_map/ppermute | solution.py:16
  169.3 7.6 %collective-permute-start.11 = (f32[2,16,2,512]{3,1,0,2:T(8,128)S(1)}, f32[2,16,2,512]{3,1,0,2:T(8,128)S(1)}, u32[]{:S(2)}, u32[]{:S(2)}) collective-permute-start(f32[2,16,2,512]{3,1,0,2:T(8,128)S(1)} %fusion.18), channel_id=1, source_target_pairs={{0,64},{4,68},{8,72},{12,76},{16,80},{20,84},{24,88},{28,92},{32,9... | collective-permute-start | bytes 393224 | tf_op jit(solution)/shard_map/ppermute | solution.py:16
  173.6 8.2 %collective-permute-start.25 = (f32[2,17,2,512]{3,1,2,0:T(8,128)S(1)}, f32[2,17,2,512]{3,1,2,0:T(8,128)S(1)}, u32[]{:S(2)}, u32[]{:S(2)}) collective-permute-start(f32[2,17,2,512]{3,1,2,0:T(8,128)S(1)} %fusion.11), channel_id=1, source_target_pairs={{0,64},{4,68},{8,72},{12,76},{16,80},{20,84},{24,88},{28,92},{32,9... | collective-permute-start | bytes 417800 | tf_op jit(solution)/shard_map/ppermute | solution.py:16
  177.0 12.1 %collective-permute-start.12 = (f32[2,16,2,512]{3,1,0,2:T(8,128)S(1)}, f32[2,16,2,512]{3,1,0,2:T(8,128)S(1)}, u32[]{:S(2)}, u32[]{:S(2)}) collective-permute-start(f32[2,16,2,512]{3,1,0,2:T(8,128)S(1)} %fusion.19), channel_id=1, source_target_pairs={{0,128},{4,132},{8,136},{12,140},{16,144},{20,148},{24,152},{28,15... | collective-permute-start | bytes 393224 | tf_op jit(solution)/shard_map/ppermute | solution.py:16
  181.9 15.6 %collective-permute-start.26 = (f32[2,17,2,512]{3,1,2,0:T(8,128)S(1)}, f32[2,17,2,512]{3,1,2,0:T(8,128)S(1)}, u32[]{:S(2)}, u32[]{:S(2)}) collective-permute-start(f32[2,17,2,512]{3,1,2,0:T(8,128)S(1)} %fusion.12), channel_id=1, source_target_pairs={{0,128},{4,132},{8,136},{12,140},{16,144},{20,148},{24,152},{28,15... | collective-permute-start | bytes 417800 | tf_op jit(solution)/shard_map/ppermute | solution.py:16
  189.2 13.1 %collective-permute-start.13 = (f32[2,16,2,512]{3,1,0,2:T(8,128)S(1)}, f32[2,16,2,512]{3,1,0,2:T(8,128)S(1)}, u32[]{:S(2)}, u32[]{:S(2)}) collective-permute-start(f32[2,16,2,512]{3,1,0,2:T(8,128)S(1)} %fusion.20), channel_id=1, source_target_pairs={{0,256},{4,260},{8,264},{12,268},{16,272},{20,276},{24,280},{28,28... | collective-permute-start | bytes 393224 | tf_op jit(solution)/shard_map/ppermute | solution.py:16
  197.6 15.6 %collective-permute-start.27 = (f32[2,17,2,512]{3,1,2,0:T(8,128)S(1)}, f32[2,17,2,512]{3,1,2,0:T(8,128)S(1)}, u32[]{:S(2)}, u32[]{:S(2)}) collective-permute-start(f32[2,17,2,512]{3,1,2,0:T(8,128)S(1)} %fusion.13), channel_id=1, source_target_pairs={{0,256},{4,260},{8,264},{12,268},{16,272},{20,276},{24,280},{28,28... | collective-permute-start | bytes 417800 | tf_op jit(solution)/shard_map/ppermute | solution.py:16
  213.6 7.3 %copy-start.5 = (f32[16]{0:T(128)S(1)}, f32[16]{0:T(128)}, u32[]{:S(2)}) copy-start(f32[16]{0:T(128)} %param.11) | copy-start | bytes 196
